TPU v7x, 512 devices: a whole 4x4x16 slice. The times are simulated.
512 devices in a mesh: leaf: 32 (over z, core), bond: 16 (over x, y).
Axes of the slice: x: 4, y: 4, z: 16, core: 2. Of those that a mesh axis runs over, the one named last changes fastest.
Arguments:
- isometries: bfloat16 [32, 256, 256, 256], P('leaf', 'bond'), may hold values from -0.1875 to 0.1875
- leaf_ops: bfloat16 [32, 1, 256, 256], P('leaf', None, 'bond'), may hold values from -6 to 6
- charges: int32 [32, 3, 4], P('leaf'), may hold values from 0 to 3
- assign: int32 [32, 1], P('leaf'), may hold values from 0 to 2
Outputs:
- node_ops: bfloat16 [32, 1, 256, 256], P('leaf', None, 'bond')
Inputs may be any that keep to these rules, and one draw needn't show every extreme that they name: `assign`: 0 takes the left child's operator, 1 the right child's, 2 their sum.
All inputs are finite; a program needn't handle non-finite values.
Results may differ from a plain program's by a relative error of at most 0.008.
Values may be sent and summed in bfloat16 or wider, within the bound.
A program may use at most 64 MiB of HBM per device.

v0:
```python
import jax
import jax.numpy as jnp
from jax import lax
from jax.sharding import PartitionSpec as P

BLOCK = 64
QMOD = 4
LEVELS = 3


def passed_along(array, axis, by):
    devices = lax.axis_size(axis)
    return lax.ppermute(array, axis, [(i, (i + by) % devices) for i in range(devices)])


def lookup(index_vector, charge_table, blocks):
    hits = index_vector[:, None] == blocks[None, :]
    return jnp.sum(jnp.where(hits, charge_table[None, :], 0), axis=1)


def shards(isometries, leaf_ops, charges, assign):
    bond_rank = lax.axis_index("bond")
    weight = isometries[0]
    slab_rows = weight.shape[0]
    bond_width = weight.shape[1]
    op_count = leaf_ops.shape[1]
    charge_row = charges[0]
    blocks = jnp.arange(charge_row.shape[1], dtype=jnp.int32)
    left_index = (bond_rank * slab_rows + jnp.arange(slab_rows, dtype=jnp.int32)) // BLOCK
    full_index = jnp.arange(bond_width, dtype=jnp.int32) // BLOCK
    charge_left = lookup(left_index, charge_row[0], blocks)
    charge_right = lookup(full_index, charge_row[1], blocks)
    charge_parent = lookup(full_index, charge_row[2], blocks)
    charge_sum = (
        charge_left[:, None, None] + charge_right[None, :, None] - charge_parent[None, None, :]
    )
    keep_mask = jnp.mod(charge_sum, QMOD) == 0
    masked = jnp.where(keep_mask, weight, jnp.zeros((), weight.dtype))
    by_right = lax.all_to_all(masked, "bond", split_axis=1, concat_axis=0, tiled=True)
    take_left = (assign[0] != 1).astype(jnp.float32)
    take_right = (assign[0] != 0).astype(jnp.float32)
    held_ops = lax.all_gather(leaf_ops[0], "bond", axis=1, tiled=True)
    for level_now in range(1, LEVELS + 1):
        reach_by = 2 ** (level_now - 1)
        left_ops = passed_along(held_ops, "leaf", reach_by)
        left_mixed = jnp.dot(
            left_ops.reshape(op_count * bond_width, bond_width),
            by_right.reshape(bond_width, -1),
            preferred_element_type=jnp.float32,
        ).astype(jnp.bfloat16)
        left_mixed = left_mixed.reshape(op_count, -1, bond_width)
        left_part = jnp.einsum(
            "rp,krq->kpq",
            by_right.reshape(-1, bond_width),
            left_mixed,
            preferred_element_type=jnp.float32,
        )
        right_mixed = jnp.einsum(
            "kcb,abq->kacq", held_ops, masked, preferred_element_type=jnp.float32
        ).astype(jnp.bfloat16)
        right_part = jnp.einsum(
            "acp,kacq->kpq", masked, right_mixed, preferred_element_type=jnp.float32
        )
        partial_sum = take_left[:, None, None] * left_part + take_right[:, None, None] * right_part
        held_ops = lax.psum(partial_sum, "bond").astype(jnp.bfloat16)
    result = lax.dynamic_slice_in_dim(held_ops, bond_rank * slab_rows, slab_rows, 1)
    return result[None]


def solution(mesh):
    in_specs = (
        P("leaf", "bond", None, None),
        P("leaf", None, "bond", None),
        P("leaf", None, None),
        P("leaf", None),
    )
    out_specs = P("leaf", None, "bond", None)
    return jax.shard_map(shards, mesh=mesh, in_specs=in_specs, out_specs=out_specs, check_vma=False)
```

profile of v0, /device:TPU:32, one launch (start us, length us, event | category | flops | bytes accessed | tf_op | source)
XLA Modules:
  0.0 344.1 jit_solution(10397409196663021548)
XLA Ops:
  0.0 0.7 slice_bitcast_fusion.2
  0.7 0.1 select_reduce_fusion.2
  0.8 0.1 select_reduce_fusion.1
  1.0 0.1 copy.50
  1.1 7.0 %fusion.6 = bf16[16,256,256]{2,0,1:T(8,128)(2,1)} fusion(bf16[1,16,256,256]{3,2,1,0:T(8,128)(2,1)} %param.4, s32[256]{0:T(256)S(1)} %get-tuple-element.6, s32[16,256]{0,1:T(8,128)S(1)} %copy.50), kind=kLoop, calls=%fused_computation.19 | loop fusion | flops 14680064 | bytes 4211712 | tf_op jit(solution)/shard_map/jit(_where)/select_n | solution.py:38
  8.0 7.2 %all-to-all-start = ((bf16[16,256,256]{2,0,1:T(8,128)(2,1)}), bf16[16,256,256]{2,0,1:T(8,128)(2,1)}, u32[]{:S(2)}, u32[]{:S(2)}) async-start(bf16[16,256,256]{2,0,1:T(8,128)(2,1)} %fusion.6), calls=%async_computation | async-start | bytes 4194304 | tf_op jit(solution)/shard_map/all_to_all | solution.py:39
  15.2 44.2 %all-gather = bf16[1,1,256,256]{3,2,1,0:T(8,128)(2,1)S(1)} all-gather(bf16[1,1,16,256]{3,2,1,0:T(8,128)(2,1)S(1)} %copy-done.3), channel_id=2, replica_groups=mesh['leaf'=32,'bond'=16] {'bond'}, dimensions={2}, use_global_device_ids=true | all-gather | bytes 139264 | tf_op jit(solution)/shard_map/all_gather | solution.py:42
  60.1 3.5 %fusion.7 = bf16[16,256,256]{2,1,0:T(8,128)(2,1)} fusion(bf16[1,16,256,256]{3,2,1,0:T(8,128)(2,1)S(1)} %copy-done, s32[256]{0:T(256)S(1)} %get-tuple-element.6, s32[16,256]{1,0:T(8,128)S(1)} %broadcast_add_fusion), kind=kLoop, calls=%fused_computation.20 | loop fusion | flops 14680064 | bytes 4211712 | tf_op jit(solution)/shard_map/jit(_where)/select_n | solution.py:38
  63.6 3.6 %fusion.26 = f32[256,256]{1,0:T(8,128)S(1)} fusion(bf16[16,256,256]{2,1,0:T(8,128)(2,1)} %fusion.7, bf16[1,1,256,256]{3,2,1,0:T(8,128)(2,1)S(1)} %all-gather, f32[]{:T(128)} %bitcast.14), kind=kOutput, calls=%fused_computation.34 | convolution fusion | flops 1074855936 | bytes 2490372 | tf_op jit(solution)/shard_map/acp,kacq->kpq/dot_general | solution.py:61
  67.2 2.5 copy.53
  69.7 0.9 copy.71
  70.6 0.4 copy-done.1
  71.0 2.1 fusion
  73.1 4.1 %copy.54 = bf16[256,4096]{1,0:T(8,128)(2,1)} copy(bf16[256,4096]{0,1:T(8,128)(2,1)} %fusion) | data formatting | bytes 4194304 | tf_op jit(solution)/shard_map/convert_element_type | solution.py:50
  77.2 4.2 %reshape.215 = bf16[4096,256]{1,0:T(8,128)(2,1)} reshape(bf16[256,4096]{1,0:T(8,128)(2,1)} %copy.54) | data formatting | bytes 4194304 | tf_op jit(solution)/shard_map/reshape.9
  81.5 3.0 fusion.46
  84.4 74.4 %all-reduce.3 = bf16[1,256,256]{1,2,0:T(8,128)(2,1)S(1)} all-reduce(f32[1,256,256]{1,2,0:T(8,128)S(1)} %fusion.46), channel_id=1, replica_groups=mesh['leaf'=32,'bond'=16] {'bond'}, use_global_device_ids=true, to_apply=%region_3.4 | all-reduce | flops 65536 | bytes 393216 | tf_op jit(solution)/shard_map/psum | solution.py:65
  158.9 4.0 %collective-permute-start.1 = (bf16[1,256,256]{1,2,0:T(8,128)(2,1)S(1)}, bf16[1,256,256]{1,2,0:T(8,128)(2,1)S(1)}, u32[]{:S(2)}, u32[]{:S(2)}) collective-permute-start(bf16[1,256,256]{1,2,0:T(8,128)(2,1)S(1)} %all-reduce.3), channel_id=1, source_target_pairs={{0,32},{16,48},{32,64},{48,80},{64,96},{80,112},{96,128},{112,144}... | collective-permute-start | bytes 393224 | tf_op jit(solution)/shard_map/ppermute | solution.py:13
  162.9 4.2 %fusion.32 = f32[256,256]{1,0:T(8,128)S(1)} fusion(bf16[16,256,256]{2,1,0:T(8,128)(2,1)} %fusion.7, bf16[1,256,256]{1,2,0:T(8,128)(2,1)S(1)} %all-reduce.3, f32[]{:T(128)} %bitcast.14), kind=kOutput, calls=%fused_computation.36 | convolution fusion | flops 1074855936 | bytes 2490372 | tf_op jit(solution)/shard_map/acp,kacq->kpq/dot_general | solution.py:61
  167.0 2.1 convolution_convert_fusion.1
  169.1 4.2 %reshape.220 = bf16[4096,256]{1,0:T(8,128)(2,1)} reshape(bf16[256,4096]{1,0:T(8,128)(2,1)} %convolution_convert_fusion.1) | data formatting | bytes 4194304 | tf_op jit(solution)/shard_map/reshape.28
  173.3 3.0 fusion.44
  176.3 71.9 %all-reduce.4 = bf16[1,256,256]{1,2,0:T(8,128)(2,1)S(1)} all-reduce(f32[1,256,256]{1,2,0:T(8,128)S(1)} %fusion.44), channel_id=1, replica_groups=mesh['leaf'=32,'bond'=16] {'bond'}, use_global_device_ids=true, to_apply=%region_4.5 | all-reduce | flops 65536 | bytes 393216 | tf_op jit(solution)/shard_map/psum | solution.py:65
  248.2 6.4 %collective-permute-start.2 = (bf16[1,256,256]{1,2,0:T(8,128)(2,1)S(1)}, bf16[1,256,256]{1,2,0:T(8,128)(2,1)S(1)}, u32[]{:S(2)}, u32[]{:S(2)}) collective-permute-start(bf16[1,256,256]{1,2,0:T(8,128)(2,1)S(1)} %all-reduce.4), channel_id=1, source_target_pairs={{0,64},{16,80},{32,96},{48,112},{64,128},{80,144},{96,160},{112,17... | collective-permute-start | bytes 393224 | tf_op jit(solution)/shard_map/ppermute | solution.py:13
  254.6 4.2 %fusion.38 = f32[256,256]{1,0:T(8,128)S(1)} fusion(bf16[16,256,256]{2,1,0:T(8,128)(2,1)} %fusion.7, bf16[1,256,256]{1,2,0:T(8,128)(2,1)S(1)} %all-reduce.4, f32[]{:T(128)} %bitcast.14), kind=kOutput, calls=%fused_computation.38 | convolution fusion | flops 1074855936 | bytes 2490372 | tf_op jit(solution)/shard_map/acp,kacq->kpq/dot_general | solution.py:61
  258.7 2.1 collective-permute-done.2
  260.9 2.1 convolution_convert_fusion
  262.9 4.4 %reshape.224 = bf16[4096,256]{1,0:T(8,128)(2,1)} reshape(bf16[256,4096]{1,0:T(8,128)(2,1)} %convolution_convert_fusion) | data formatting | bytes 4194304 | tf_op jit(solution)/shard_map/reshape.35
  267.3 2.3 fusion.42
  269.6 73.7 %all-reduce.5 = bf16[1,256,256]{1,2,0:T(8,128)(2,1)S(1)} all-reduce(f32[1,256,256]{1,2,0:T(8,128)S(1)} %fusion.42), channel_id=1, replica_groups=mesh['leaf'=32,'bond'=16] {'bond'}, use_global_device_ids=true, to_apply=%region_5.6 | all-reduce | flops 65536 | bytes 393216 | tf_op jit(solution)/shard_map/psum | solution.py:65
  343.3 0.1 dynamic-slice_convert_fusion
  343.4 0.7 copy.61
  (14 shorter events, 0.1 us)
Async XLA Ops:
  8.0 7.2 %copy-start.3 = (bf16[1,1,16,256]{3,2,1,0:T(8,128)(2,1)S(1)}, bf16[1,1,16,256]{3,2,1,0:T(8,128)(2,1)}, u32[]{:S(2)}) copy-start(bf16[1,1,16,256]{3,2,1,0:T(8,128)(2,1)} %param.5) | copy-start | bytes 24580
  8.0 52.1 %copy-start = (bf16[1,16,256,256]{3,2,1,0:T(8,128)(2,1)S(1)}, bf16[1,16,256,256]{3,2,1,0:T(8,128)(2,1)}, u32[]{:S(2)}) copy-start(bf16[1,16,256,256]{3,2,1,0:T(8,128)(2,1)} %param.4) | copy-start | bytes 6291460
  8.0 59.2 %all-to-all-start = ((bf16[16,256,256]{2,0,1:T(8,128)(2,1)}), bf16[16,256,256]{2,0,1:T(8,128)(2,1)}, u32[]{:S(2)}, u32[]{:S(2)}) async-start(bf16[16,256,256]{2,0,1:T(8,128)(2,1)} %fusion.6), calls=%async_computation | async-start | bytes 4194304 | tf_op jit(solution)/shard_map/all_to_all | solution.py:39
  59.4 11.6 %collective-permute-start = (bf16[1,256,256]{2,1,0:T(8,128)(2,1)S(1)}, bf16[1,256,256]{2,1,0:T(8,128)(2,1)S(1)}, u32[]{:S(2)}, u32[]{:S(2)}) collective-permute-start(bf16[1,256,256]{2,1,0:T(8,128)(2,1)S(1)} %bitcast.131), channel_id=1, source_target_pairs={{0,16},{16,32},{32,48},{48,64},{64,80},{80,96},{96,112},{112,128},... | collective-permute-start | bytes 393224 | tf_op jit(solution)/shard_map/ppermute | solution.py:13
  69.7 1.3 copy-start.1
  158.9 8.2 %collective-permute-start.1 = (bf16[1,256,256]{1,2,0:T(8,128)(2,1)S(1)}, bf16[1,256,256]{1,2,0:T(8,128)(2,1)S(1)}, u32[]{:S(2)}, u32[]{:S(2)}) collective-permute-start(bf16[1,256,256]{1,2,0:T(8,128)(2,1)S(1)} %all-reduce.3), channel_id=1, source_target_pairs={{0,32},{16,48},{32,64},{48,80},{64,96},{80,112},{96,128},{112,144}... | collective-permute-start | bytes 393224 | tf_op jit(solution)/shard_map/ppermute | solution.py:13
  248.2 12.7 %collective-permute-start.2 = (bf16[1,256,256]{1,2,0:T(8,128)(2,1)S(1)}, bf16[1,256,256]{1,2,0:T(8,128)(2,1)S(1)}, u32[]{:S(2)}, u32[]{:S(2)}) collective-permute-start(bf16[1,256,256]{1,2,0:T(8,128)(2,1)S(1)} %all-reduce.4), channel_id=1, source_target_pairs={{0,64},{16,80},{32,96},{48,112},{64,128},{80,144},{96,160},{112,17... | collective-permute-start | bytes 393224 | tf_op jit(solution)/shard_map/ppermute | solution.py:13
  262.9 4.4 %copy-start.2 = (bf16[16,16,16,256]{3,2,1,0:T(8,128)(2,1)S(1)}, bf16[16,16,16,256]{3,2,1,0:T(8,128)(2,1)}, u32[]{:S(2)}) copy-start(bf16[16,16,16,256]{3,2,1,0:T(8,128)(2,1)} %copy-done.1) | copy-start | bytes 6291460
where the time goes:
time: 345 us; the launch traced here: 344 us
  blocking collectives  264 us (77%)
  matrix products  26.4 us (8%)
  local copies, waits for them, and re-layouts  22.3 us (6%)
  starting transfers between devices  17.6 us (5%)
  other arithmetic  10.7 us (3%)
    psum x3, blocking collectives, shards(): held_ops = lax.psum(partial_sum, 'bond').astype(jnp.bfloat16)  220 us
    all_gather x1, blocking collectives, shards(): held_ops = lax.all_gather(leaf_ops[0], 'bond', axis=1, tiled=True)  44.2 us
    another operation x3, local copies, waits for them, and re-layouts  12.8 us
    dot_general x3, matrix products, shards(): jnp.einsum('acp,kacq->kpq', masked, right_mixed, preferred_element_type=j...  11.9 us
    select_n x2, other arithmetic, shards(): masked = jnp.where(keep_mask, weight, jnp.zeros((), weight.dtype))  10.4 us
    ppermute x3, starting transfers between devices, passed_along(): lax.ppermute(array, axis, [(i, (i + by) % devices) for i in range(devices)])  10.4 us
    dot_general x3, matrix products, shards(): jnp.einsum('rp,krq->kpq', by_right.reshape(-1, bond_width), left_mixed, p...  8.27 us
    all_to_all x1, starting transfers between devices, shards(): lax.all_to_all(masked, 'bond', split_axis=1, concat_axis=0, tiled=True)  7.22 us
  transfers between devices with their start and end apart: 4, of which 1 were waited for; matrix products, arithmetic and copies ran while one was open for 5% of the time, Pallas kernels for 0%

commit v1 on v0

v1 whole, which is shorter than its diff:
```python
import functools

import jax
import jax.numpy as jnp
from jax import lax
from jax.experimental import pallas as pl
from jax.experimental.pallas import tpu as pltpu
from jax.sharding import PartitionSpec as P

NBLK = 4
LEVELS = 3
CHUNKS = 4
BF = jnp.bfloat16
F32 = jnp.float32
MESH = pl.DeviceIdType.MESH


def dot(a, b):
    return jnp.dot(a, b, preferred_element_type=F32)


def kernel(
    n, leaves, iso, leaf_op, charges, assign, out,
    mm, sendb, mb, vt, ut, mask, perm, scaled, acc, xs, rbuf, lbuf, zbuf, rss, rsr,
    load_sem, a2a_send, a2a_recv, r_send, r_recv, l_send, l_recv, z_send, z_recv, s_send, s_recv,
):
    slab, chi, _ = iso.shape
    block = chi // NBLK
    per = slab // CHUNKS
    me = lax.axis_index("bond")
    slot = lax.axis_index("leaf")

    def peer(off):
        return lax.rem(me + off, n)

    def ahead(by):
        return lax.rem(slot + by, leaves)

    def rows(i):
        return pl.ds(pl.multiple_of(i * slab, slab), slab)

    mine = rows(me)

    load = pltpu.make_async_copy(iso, mm, load_sem)
    load.start()

    barrier = pltpu.get_barrier_semaphore()

    def greet(off, carry):
        pl.semaphore_signal(barrier, inc=1, device_id=(slot, peer(off)), device_id_type=MESH)
        return carry

    lax.fori_loop(1, n, greet, 0)
    for level in range(LEVELS):
        for by in (2**level, leaves - 2**level):
            pl.semaphore_signal(barrier, inc=1, device_id=(ahead(by), me), device_id_type=MESH)

    row_block = lax.broadcasted_iota(jnp.int32, (chi, chi), 0) // block
    col_block = lax.broadcasted_iota(jnp.int32, (chi, chi), 1) // block
    total = jnp.zeros((chi, chi), jnp.int32) + charges[0, (me * slab) // block]
    for k in range(NBLK):
        total = total + jnp.where(row_block == k, charges[1, k], 0) - jnp.where(col_block == k, charges[2, k], 0)
    mask[...] = jnp.where((total & 3) == 0, 1.0, 0.0).astype(BF)

    side = slab * slab
    to = lax.broadcasted_iota(jnp.int32, (side, side), 0)
    frm = lax.broadcasted_iota(jnp.int32, (side, side), 1)
    perm[...] = jnp.where((to // slab == frm % slab) & (to % slab == frm // slab), 1.0, 0.0).astype(BF)

    load.wait()

    def prepare(e, carry):
        piece = mm[:, rows(e), :] * mask[rows(e), :][None]
        mm[:, rows(e), :] = piece
        turned = dot(perm[...], piece.reshape(side, chi)).astype(BF)
        sendb[e] = turned.reshape(slab, slab, chi)
        return carry

    lax.fori_loop(0, n, prepare, 0)
    mb[:, mine, :] = sendb[me]

    pl.semaphore_wait(barrier, n - 1 + 2 * LEVELS)

    def spread(src, dst, level, send, recv):
        def go(off, carry):
            pltpu.make_async_remote_copy(
                src_ref=src, dst_ref=dst.at[level, mine], send_sem=send.at[level], recv_sem=recv.at[level],
                device_id=(slot, peer(off)), device_id_type=MESH,
            ).start()
            return carry

        lax.fori_loop(1, n, go, 0)

    def drain(ref, sem):
        pltpu.make_async_copy(ref, ref, sem).wait()

    others = pl.ds(0, chi - slab)

    def hand_on(src, level):
        return pltpu.make_async_remote_copy(
            src_ref=src, dst_ref=zbuf.at[level], send_sem=z_send.at[level], recv_sem=z_recv.at[level],
            device_id=(ahead(2**level), me), device_id_type=MESH,
        )

    def publish(src, level):
        hand_on(src, level).start()
        rbuf[level, mine] = src[...]
        spread(src, rbuf, level, r_send, r_recv)

    def forward(src, level):
        hand_on(src, level).wait_recv()
        lbuf[level, mine] = zbuf[level]
        spread(zbuf.at[level], lbuf, level, l_send, l_recv)

    def exchange(c):
        part = pl.ds(c * per, per)

        def go(off, carry):
            to_dev = peer(off)
            pltpu.make_async_remote_copy(
                src_ref=sendb.at[to_dev, part], dst_ref=mb.at[part, mine],
                send_sem=a2a_send.at[c], recv_sem=a2a_recv.at[c],
                device_id=(slot, to_dev), device_id_type=MESH,
            ).start()
            return carry

        lax.fori_loop(1, n, go, 0)

    publish(leaf_op, 0)
    exchange(0)
    forward(leaf_op, 0)
    for c in range(1, CHUNKS):
        exchange(c)

    def flip(a, carry):
        vt[a] = mm[a].T
        return carry

    lax.fori_loop(0, slab, flip, 0)

    take_left = jnp.where(assign[0] != 1, 1.0, 0.0).astype(BF)
    take_right = jnp.where(assign[0] != 0, 1.0, 0.0).astype(BF)

    def contract(turned, plain, first, count):
        def step(i, carry):
            mixed = dot(turned[i], scaled[...]).astype(BF)
            acc[...] += dot(mixed, plain[i])
            return carry

        lax.fori_loop(first, first + count, step, 0)

    for level in range(LEVELS):
        drain(rbuf.at[level, others], r_recv.at[level])
        scaled[...] = rbuf[level] * take_right
        acc[...] = jnp.zeros_like(acc)
        if level > 0:
            forward(xs.at[level - 1], level)
        contract(vt, mm, 0, slab)
        drain(lbuf.at[level, others], l_recv.at[level])
        scaled[...] = lbuf[level] * take_left
        if level == 0:
            for c in range(CHUNKS):
                drain(mb.at[pl.ds(c * per, per), others], a2a_recv.at[c])

                def turn(b, carry):
                    ut[b] = mb[b].T
                    return carry

                lax.fori_loop(c * per, (c + 1) * per, turn, 0)
                contract(ut, mb, c * per, per)
        else:
            contract(ut, mb, 0, slab)

        rss[level] = acc[...].astype(BF)
        rsr[level, me] = rss[level, mine]

        def scatter(off, carry):
            to_dev = peer(off)
            pltpu.make_async_remote_copy(
                src_ref=rss.at[level, rows(to_dev)], dst_ref=rsr.at[level, me],
                send_sem=s_send.at[level], recv_sem=s_recv.at[level],
                device_id=(slot, to_dev), device_id_type=MESH,
            ).start()
            return carry

        lax.fori_loop(1, n, scatter, 0)
        drain(rsr.at[level, pl.ds(0, n - 1)], s_recv.at[level])
        whole = rsr[level, 0].astype(F32)
        for i in range(1, n):
            whole = whole + rsr[level, i].astype(F32)
        if level < LEVELS - 1:
            xs[level] = whole.astype(BF)
            publish(xs.at[level], level + 1)
        else:
            out[...] = whole.astype(BF)

    for c in range(CHUNKS):
        drain(mb.at[pl.ds(c * per, per), others], a2a_send.at[c])
    for level in range(LEVELS):
        drain(rbuf.at[level, others], r_send.at[level])
        drain(lbuf.at[level, others], l_send.at[level])
        drain(zbuf.at[level], z_send.at[level])
        drain(rsr.at[level, pl.ds(0, n - 1)], s_send.at[level])


def shards(isometries, leaf_ops, charges, assign):
    iso = isometries[0]
    slab, chi, _ = iso.shape
    n = lax.axis_size("bond")
    leaves = lax.axis_size("leaf")
    sem = pltpu.SemaphoreType.DMA
    result = pl.pallas_call(
        functools.partial(kernel, n, leaves),
        out_shape=jax.ShapeDtypeStruct((slab, chi), BF),
        in_specs=[
            pl.BlockSpec(memory_space=pl.ANY),
            pl.BlockSpec(memory_space=pltpu.VMEM),
            pl.BlockSpec(memory_space=pltpu.SMEM),
            pl.BlockSpec(memory_space=pltpu.SMEM),
        ],
        out_specs=pl.BlockSpec(memory_space=pltpu.VMEM),
        scratch_shapes=[
            pltpu.VMEM((slab, chi, chi), BF),
            pltpu.VMEM((n, slab, slab, chi), BF),
            pltpu.VMEM((slab, chi, chi), BF),
            pltpu.VMEM((slab, chi, chi), BF),
            pltpu.VMEM((slab, chi, chi), BF),
            pltpu.VMEM((chi, chi), BF),
            pltpu.VMEM((slab * slab, slab * slab), BF),
            pltpu.VMEM((chi, chi), BF),
            pltpu.VMEM((chi, chi), F32),
            pltpu.VMEM((LEVELS, slab, chi), BF),
            pltpu.VMEM((LEVELS, chi, chi), BF),
            pltpu.VMEM((LEVELS, chi, chi), BF),
            pltpu.VMEM((LEVELS, slab, chi), BF),
            pltpu.VMEM((LEVELS, chi, chi), BF),
            pltpu.VMEM((LEVELS, n, slab, chi), BF),
            sem,
            sem((CHUNKS,)), sem((CHUNKS,)),
            sem((LEVELS,)), sem((LEVELS,)),
            sem((LEVELS,)), sem((LEVELS,)),
            sem((LEVELS,)), sem((LEVELS,)),
            sem((LEVELS,)), sem((LEVELS,)),
        ],
        compiler_params=pltpu.CompilerParams(collective_id=0, has_side_effects=True),
    )(iso, leaf_ops[0, 0], charges[0], assign[0])
    return result[None, None]


def solution(mesh):
    in_specs = (
        P("leaf", "bond", None, None),
        P("leaf", None, "bond", None),
        P("leaf", None, None),
        P("leaf", None),
    )
    out_specs = P("leaf", None, "bond", None)
    return jax.shard_map(shards, mesh=mesh, in_specs=in_specs, out_specs=out_specs, check_vma=False)
```

time: 345 us -> 96.5 us (0.28)
  the two profiles are of different devices: /device:TPU:32 before, /device:TPU:8 now
where the time goes in v1:
time: 96.5 us; the launch traced here: 96.3 us
  Pallas kernels  93 us (96%)
  local copies, waits for them, and re-layouts  2.56 us (3%)
    pallas_call x1, Pallas kernels, shards(): pl.pallas_call(functools.partial(kernel, n, leaves), out_shape=jax.ShapeD...  93 us
    unnamed x2, local copies, waits for them, and re-layouts  2.56 us

profile of v1, /device:TPU:8, one launch (start us, length us, event | category | flops | bytes accessed | tf_op | source)
XLA Modules:
  0.0 96.3 jit_solution(9729456767153020956)
XLA Ops:
  0.7 1.3 %copy.7 = s32[1,3,4]{2,1,0:T(4,128)} copy(s32[1,3,4]{2,0,1:T(1,128)} %param.6) | data formatting | bytes 96
  1.9 93.0 %shard_map.46 = bf16[16,256]{1,0:T(8,128)(2,1)} custom-call(bf16[16,256,256]{2,1,0:T(8,128)(2,1)} %bitcast.8, bf16[16,256]{1,0:T(8,128)(2,1)} %bitcast.10, s32[3,4]{1,0:T(4,128)} %bitcast.11, s32[1]{0:T(128)} %bitcast.7.assign), custom_call_target="tpu_custom_call" | custom-call | tf_op jit(solution)/shard_map/pallas_call | solution.py:212
  95.0 1.3 %copy.10 = bf16[1,1,16,256]{3,2,1,0:T(8,128)(2,1)} copy(bf16[1,1,16,256]{3,2,1,0:T(8,128)(2,1)} %bitcast.9) | data formatting | bytes 16384

commit v2 on v1

--- a/solution.py
+++ b/solution.py
@@ -52,14 +52,13 @@
 
     lax.fori_loop(1, n, greet, 0)
     for level in range(LEVELS):
-        for by in (2**level, leaves - 2**level):
-            pl.semaphore_signal(barrier, inc=1, device_id=(ahead(by), me), device_id_type=MESH)
+        pl.semaphore_signal(barrier, inc=1, device_id=(ahead(leaves - 2**level), me), device_id_type=MESH)
 
     row_block = lax.broadcasted_iota(jnp.int32, (chi, chi), 0) // block
     col_block = lax.broadcasted_iota(jnp.int32, (chi, chi), 1) // block
-    total = jnp.zeros((chi, chi), jnp.int32) + charges[0, (me * slab) // block]
+    total = jnp.zeros((chi, chi), jnp.int32) + charges[0, 0, (me * slab) // block]
     for k in range(NBLK):
-        total = total + jnp.where(row_block == k, charges[1, k], 0) - jnp.where(col_block == k, charges[2, k], 0)
+        total = total + jnp.where(row_block == k, charges[1, 0, k], 0) - jnp.where(col_block == k, charges[2, 0, k], 0)
     mask[...] = jnp.where((total & 3) == 0, 1.0, 0.0).astype(BF)
 
     side = slab * slab
@@ -76,10 +75,10 @@
         sendb[e] = turned.reshape(slab, slab, chi)
         return carry
 
-    lax.fori_loop(0, n, prepare, 0)
+    lax.fori_loop(0, n, prepare, 0, unroll=4)
     mb[:, mine, :] = sendb[me]
 
-    pl.semaphore_wait(barrier, n - 1 + 2 * LEVELS)
+    pl.semaphore_wait(barrier, n - 1 + LEVELS)
 
     def spread(src, dst, level, send, recv):
         def go(off, carry):
@@ -136,7 +135,7 @@
         vt[a] = mm[a].T
         return carry
 
-    lax.fori_loop(0, slab, flip, 0)
+    lax.fori_loop(0, slab, flip, 0, unroll=4)
 
     take_left = jnp.where(assign[0] != 1, 1.0, 0.0).astype(BF)
     take_right = jnp.where(assign[0] != 0, 1.0, 0.0).astype(BF)
@@ -147,14 +146,14 @@
             acc[...] += dot(mixed, plain[i])
             return carry
 
-        lax.fori_loop(first, first + count, step, 0)
+        lax.fori_loop(first, first + count, step, 0, unroll=True)
 
     for level in range(LEVELS):
+        if level > 0:
+            forward(xs.at[level - 1], level)
         drain(rbuf.at[level, others], r_recv.at[level])
         scaled[...] = rbuf[level] * take_right
         acc[...] = jnp.zeros_like(acc)
-        if level > 0:
-            forward(xs.at[level - 1], level)
         contract(vt, mm, 0, slab)
         drain(lbuf.at[level, others], l_recv.at[level])
         scaled[...] = lbuf[level] * take_left
@@ -166,7 +165,7 @@
                     ut[b] = mb[b].T
                     return carry
 
-                lax.fori_loop(c * per, (c + 1) * per, turn, 0)
+                lax.fori_loop(c * per, (c + 1) * per, turn, 0, unroll=True)
                 contract(ut, mb, c * per, per)
         else:
             contract(ut, mb, 0, slab)
@@ -243,7 +242,7 @@
             sem((LEVELS,)), sem((LEVELS,)),
         ],
         compiler_params=pltpu.CompilerParams(collective_id=0, has_side_effects=True),
-    )(iso, leaf_ops[0, 0], charges[0], assign[0])
+    )(iso, leaf_ops[0, 0], jnp.transpose(charges, (1, 0, 2)), assign[0])
     return result[None, None]
 
 

time: 96.5 us -> 81.8 us (0.85)
  Pallas kernels: 93 us -> 79.6 us
  local copies, waits for them, and re-layouts: 2.56 us -> 1.3 us
    pallas_call x1, Pallas kernels: 93 us -> 79.6 us  [shards(): pl.pallas_call(functools.partial(kernel, n, leaves), out_shape=jax.ShapeD...]
    unnamed x2 -> x1, local copies, waits for them, and re-layouts: 2.56 us -> 1.3 us
where the time goes in v2:
time: 81.8 us; the launch traced here: 81.6 us
  Pallas kernels  79.6 us (97%)
  local copies, waits for them, and re-layouts  1.3 us (2%)
    pallas_call x1, Pallas kernels, shards(): pl.pallas_call(functools.partial(kernel, n, leaves), out_shape=jax.ShapeD...  79.6 us

profile of v2, /device:TPU:8, one launch (start us, length us, event | category | flops | bytes accessed | tf_op | source)
XLA Modules:
  0.0 81.6 jit_solution(11074038239044413105)
XLA Ops:
  0.7 79.6 %shard_map.46 = bf16[16,256]{1,0:T(8,128)(2,1)} custom-call(bf16[16,256,256]{2,1,0:T(8,128)(2,1)} %bitcast.6, bf16[16,256]{1,0:T(8,128)(2,1)} %bitcast.8, s32[3,1,4]{2,1,0:T(1,128)} %bitcast.9, s32[1]{0:T(128)} %bitcast.5.assign), custom_call_target="tpu_custom_call" | custom-call | tf_op jit(solution)/shard_map/pallas_call | solution.py:211
  80.3 1.3 %copy.7 = bf16[1,1,16,256]{3,2,1,0:T(8,128)(2,1)} copy(bf16[1,1,16,256]{3,2,1,0:T(8,128)(2,1)} %bitcast.7) | data formatting | bytes 16384

commit v3 on v2

--- a/solution.py
+++ b/solution.py
@@ -1,4 +1,5 @@
 import functools
+import math
 
 import jax
 import jax.numpy as jnp
@@ -30,8 +31,15 @@
     me = lax.axis_index("bond")
     slot = lax.axis_index("leaf")
 
-    def peer(off):
-        return lax.rem(me + off, n)
+    width = math.isqrt(n)
+    steps = sorted(
+        ((i, j) for i in range(width) for j in range(width)),
+        key=lambda at: -sum(min(k, width - k) for k in at),
+    )
+    others_at = steps[:-1]
+
+    def peer(at):
+        return lax.rem(me // width + at[0], width) * width + lax.rem(lax.rem(me, width) + at[1], width)
 
     def ahead(by):
         return lax.rem(slot + by, leaves)
@@ -46,13 +54,14 @@
 
     barrier = pltpu.get_barrier_semaphore()
 
-    def greet(off, carry):
-        pl.semaphore_signal(barrier, inc=1, device_id=(slot, peer(off)), device_id_type=MESH)
-        return carry
-
-    lax.fori_loop(1, n, greet, 0)
-    for level in range(LEVELS):
-        pl.semaphore_signal(barrier, inc=1, device_id=(ahead(leaves - 2**level), me), device_id_type=MESH)
+    for at in others_at:
+        pl.semaphore_signal(barrier, inc=1, device_id=(slot, peer(at)), device_id_type=MESH)
+    pl.semaphore_signal(barrier, inc=1, device_id=(ahead(leaves - 1), me), device_id_type=MESH)
+    for level in range(1, LEVELS):
+        for at in steps:
+            pl.semaphore_signal(
+                barrier, inc=1, device_id=(ahead(leaves - 2**level), peer(at)), device_id_type=MESH
+            )
 
     row_block = lax.broadcasted_iota(jnp.int32, (chi, chi), 0) // block
     col_block = lax.broadcasted_iota(jnp.int32, (chi, chi), 1) // block
@@ -78,56 +87,50 @@
     lax.fori_loop(0, n, prepare, 0, unroll=4)
     mb[:, mine, :] = sendb[me]
 
-    pl.semaphore_wait(barrier, n - 1 + LEVELS)
-
-    def spread(src, dst, level, send, recv):
-        def go(off, carry):
-            pltpu.make_async_remote_copy(
-                src_ref=src, dst_ref=dst.at[level, mine], send_sem=send.at[level], recv_sem=recv.at[level],
-                device_id=(slot, peer(off)), device_id_type=MESH,
-            ).start()
-            return carry
-
-        lax.fori_loop(1, n, go, 0)
+    pl.semaphore_wait(barrier, n + n * (LEVELS - 1))
+
+    def post(src, dst, level, send, recv, to_slot, at):
+        pltpu.make_async_remote_copy(
+            src_ref=src, dst_ref=dst.at[level, mine], send_sem=send.at[level], recv_sem=recv.at[level],
+            device_id=(to_slot, peer(at)), device_id_type=MESH,
+        ).start()
 
     def drain(ref, sem):
         pltpu.make_async_copy(ref, ref, sem).wait()
 
     others = pl.ds(0, chi - slab)
 
-    def hand_on(src, level):
-        return pltpu.make_async_remote_copy(
-            src_ref=src, dst_ref=zbuf.at[level], send_sem=z_send.at[level], recv_sem=z_recv.at[level],
-            device_id=(ahead(2**level), me), device_id_type=MESH,
-        )
+    hand_on = pltpu.make_async_remote_copy(
+        src_ref=leaf_op, dst_ref=zbuf, send_sem=z_send, recv_sem=z_recv,
+        device_id=(ahead(1), me), device_id_type=MESH,
+    )
 
     def publish(src, level):
-        hand_on(src, level).start()
+        for at in steps:
+            if level > 0:
+                post(src, lbuf, level, l_send, l_recv, ahead(2**level), at)
+            if at != (0, 0):
+                post(src, rbuf, level, r_send, r_recv, slot, at)
         rbuf[level, mine] = src[...]
-        spread(src, rbuf, level, r_send, r_recv)
-
-    def forward(src, level):
-        hand_on(src, level).wait_recv()
-        lbuf[level, mine] = zbuf[level]
-        spread(zbuf.at[level], lbuf, level, l_send, l_recv)
 
     def exchange(c):
         part = pl.ds(c * per, per)
 
-        def go(off, carry):
-            to_dev = peer(off)
+        for at in others_at:
+            to_dev = peer(at)
             pltpu.make_async_remote_copy(
                 src_ref=sendb.at[to_dev, part], dst_ref=mb.at[part, mine],
                 send_sem=a2a_send.at[c], recv_sem=a2a_recv.at[c],
                 device_id=(slot, to_dev), device_id_type=MESH,
             ).start()
-            return carry
-
-        lax.fori_loop(1, n, go, 0)
-
+
+    hand_on.start()
     publish(leaf_op, 0)
     exchange(0)
-    forward(leaf_op, 0)
+    hand_on.wait_recv()
+    lbuf[0, mine] = zbuf[...]
+    for at in others_at:
+        post(zbuf, lbuf, 0, l_send, l_recv, slot, at)
     for c in range(1, CHUNKS):
         exchange(c)
 
@@ -149,13 +152,11 @@
         lax.fori_loop(first, first + count, step, 0, unroll=True)
 
     for level in range(LEVELS):
-        if level > 0:
-            forward(xs.at[level - 1], level)
         drain(rbuf.at[level, others], r_recv.at[level])
         scaled[...] = rbuf[level] * take_right
         acc[...] = jnp.zeros_like(acc)
         contract(vt, mm, 0, slab)
-        drain(lbuf.at[level, others], l_recv.at[level])
+        drain(lbuf.at[level] if level > 0 else lbuf.at[level, others], l_recv.at[level])
         scaled[...] = lbuf[level] * take_left
         if level == 0:
             for c in range(CHUNKS):
@@ -171,18 +172,14 @@
             contract(ut, mb, 0, slab)
 
         rss[level] = acc[...].astype(BF)
-        rsr[level, me] = rss[level, mine]
-
-        def scatter(off, carry):
-            to_dev = peer(off)
+        for at in others_at:
+            to_dev = peer(at)
             pltpu.make_async_remote_copy(
                 src_ref=rss.at[level, rows(to_dev)], dst_ref=rsr.at[level, me],
                 send_sem=s_send.at[level], recv_sem=s_recv.at[level],
                 device_id=(slot, to_dev), device_id_type=MESH,
             ).start()
-            return carry
-
-        lax.fori_loop(1, n, scatter, 0)
+        rsr[level, me] = rss[level, mine]
         drain(rsr.at[level, pl.ds(0, n - 1)], s_recv.at[level])
         whole = rsr[level, 0].astype(F32)
         for i in range(1, n):
@@ -193,12 +190,12 @@
         else:
             out[...] = whole.astype(BF)
 
+    hand_on.wait_send()
     for c in range(CHUNKS):
         drain(mb.at[pl.ds(c * per, per), others], a2a_send.at[c])
     for level in range(LEVELS):
         drain(rbuf.at[level, others], r_send.at[level])
-        drain(lbuf.at[level, others], l_send.at[level])
-        drain(zbuf.at[level], z_send.at[level])
+        drain(lbuf.at[level] if level > 0 else lbuf.at[level, others], l_send.at[level])
         drain(rsr.at[level, pl.ds(0, n - 1)], s_send.at[level])
 
 
@@ -231,14 +228,14 @@
             pltpu.VMEM((LEVELS, slab, chi), BF),
             pltpu.VMEM((LEVELS, chi, chi), BF),
             pltpu.VMEM((LEVELS, chi, chi), BF),
-            pltpu.VMEM((LEVELS, slab, chi), BF),
+            pltpu.VMEM((slab, chi), BF),
             pltpu.VMEM((LEVELS, chi, chi), BF),
             pltpu.VMEM((LEVELS, n, slab, chi), BF),
             sem,
             sem((CHUNKS,)), sem((CHUNKS,)),
             sem((LEVELS,)), sem((LEVELS,)),
             sem((LEVELS,)), sem((LEVELS,)),
-            sem((LEVELS,)), sem((LEVELS,)),
+            sem, sem,
             sem((LEVELS,)), sem((LEVELS,)),
         ],
         compiler_params=pltpu.CompilerParams(collective_id=0, has_side_effects=True),

time: 81.8 us -> 76.3 us (0.933)
  the two profiles are of different devices: /device:TPU:8 before, /device:TPU:2 now
where the time goes in v3:
time: 76.3 us; the launch traced here: 76.1 us
  Pallas kernels  74.1 us (97%)
  local copies, waits for them, and re-layouts  1.3 us (2%)
    pallas_call x1, Pallas kernels, shards(): pl.pallas_call(functools.partial(kernel, n, leaves), out_shape=jax.ShapeD...  74.1 us

profile of v3, /device:TPU:2, one launch (start us, length us, event | category | flops | bytes accessed | tf_op | source)
XLA Modules:
  0.0 76.1 jit_solution(17228997649144107117)
XLA Ops:
  0.7 74.1 %shard_map.46 = bf16[16,256]{1,0:T(8,128)(2,1)} custom-call(bf16[16,256,256]{2,1,0:T(8,128)(2,1)} %bitcast.6, bf16[16,256]{1,0:T(8,128)(2,1)} %bitcast.8, s32[3,1,4]{2,1,0:T(1,128)} %bitcast.9, s32[1]{0:T(128)} %bitcast.5.assign), custom_call_target="tpu_custom_call" | custom-call | tf_op jit(solution)/shard_map/pallas_call | solution.py:208
  74.8 1.3 %copy.7 = bf16[1,1,16,256]{3,2,1,0:T(8,128)(2,1)} copy(bf16[1,1,16,256]{3,2,1,0:T(8,128)(2,1)} %bitcast.7) | data formatting | bytes 16384

commit v4 on v3

--- a/solution.py
+++ b/solution.py
@@ -21,9 +21,9 @@
 
 
 def kernel(
-    n, leaves, iso, leaf_op, charges, assign, out,
-    mm, sendb, mb, vt, ut, mask, perm, scaled, acc, xs, rbuf, lbuf, zbuf, rss, rsr,
-    load_sem, a2a_send, a2a_recv, r_send, r_recv, l_send, l_recv, z_send, z_recv, s_send, s_recv,
+    n, leaves, iso, leaf_hbm, charges, assign, out,
+    leaf_op, mm, sendb, mb, vt, ut, mask, perm, scaled, acc, xs, rbuf, lbuf, zbuf, rss, rsr,
+    load_sem, leaf_sem, a2a_send, a2a_recv, r_send, r_recv, l_send, l_recv, z_send, z_recv, s_send, s_recv,
 ):
     slab, chi, _ = iso.shape
     block = chi // NBLK
@@ -51,6 +51,8 @@
 
     load = pltpu.make_async_copy(iso, mm, load_sem)
     load.start()
+    load_leaf = pltpu.make_async_copy(leaf_hbm, leaf_op, leaf_sem)
+    load_leaf.start()
 
     barrier = pltpu.get_barrier_semaphore()
 
@@ -76,6 +78,7 @@
     perm[...] = jnp.where((to // slab == frm % slab) & (to % slab == frm // slab), 1.0, 0.0).astype(BF)
 
     load.wait()
+    load_leaf.wait()
 
     def prepare(e, carry):
         piece = mm[:, rows(e), :] * mask[rows(e), :][None]
@@ -116,7 +119,7 @@
     def exchange(c):
         part = pl.ds(c * per, per)
 
-        for at in others_at:
+        for at in reversed(others_at):
             to_dev = peer(at)
             pltpu.make_async_remote_copy(
                 src_ref=sendb.at[to_dev, part], dst_ref=mb.at[part, mine],
@@ -124,21 +127,10 @@
                 device_id=(slot, to_dev), device_id_type=MESH,
             ).start()
 
-    hand_on.start()
-    publish(leaf_op, 0)
-    exchange(0)
-    hand_on.wait_recv()
-    lbuf[0, mine] = zbuf[...]
-    for at in others_at:
-        post(zbuf, lbuf, 0, l_send, l_recv, slot, at)
-    for c in range(1, CHUNKS):
-        exchange(c)
-
     def flip(a, carry):
         vt[a] = mm[a].T
         return carry
 
-    lax.fori_loop(0, slab, flip, 0, unroll=4)
 
     take_left = jnp.where(assign[0] != 1, 1.0, 0.0).astype(BF)
     take_right = jnp.where(assign[0] != 0, 1.0, 0.0).astype(BF)
@@ -151,11 +143,29 @@
 
         lax.fori_loop(first, first + count, step, 0, unroll=True)
 
-    for level in range(LEVELS):
+    def right_part(level):
         drain(rbuf.at[level, others], r_recv.at[level])
         scaled[...] = rbuf[level] * take_right
         acc[...] = jnp.zeros_like(acc)
         contract(vt, mm, 0, slab)
+
+    hand_on.start()
+    publish(leaf_op, 0)
+    exchange(0)
+    exchange(1)
+    lax.fori_loop(0, slab, flip, 0, unroll=4)
+    hand_on.wait_recv()
+    lbuf[0, mine] = zbuf[...]
+    for at in others_at:
+        post(zbuf, lbuf, 0, l_send, l_recv, slot, at)
+    exchange(2)
+    right_part(0)
+    for c in range(3, CHUNKS):
+        exchange(c)
+
+    for level in range(LEVELS):
+        if level > 0:
+            right_part(level)
         drain(lbuf.at[level] if level > 0 else lbuf.at[level, others], l_recv.at[level])
         scaled[...] = lbuf[level] * take_left
         if level == 0:
@@ -188,7 +198,7 @@
             xs[level] = whole.astype(BF)
             publish(xs.at[level], level + 1)
         else:
-            out[...] = whole.astype(BF)
+            out[...] = whole
 
     hand_on.wait_send()
     for c in range(CHUNKS):
@@ -207,15 +217,16 @@
     sem = pltpu.SemaphoreType.DMA
     result = pl.pallas_call(
         functools.partial(kernel, n, leaves),
-        out_shape=jax.ShapeDtypeStruct((slab, chi), BF),
+        out_shape=jax.ShapeDtypeStruct((slab, chi), F32),
         in_specs=[
             pl.BlockSpec(memory_space=pl.ANY),
-            pl.BlockSpec(memory_space=pltpu.VMEM),
+            pl.BlockSpec(memory_space=pl.ANY),
             pl.BlockSpec(memory_space=pltpu.SMEM),
             pl.BlockSpec(memory_space=pltpu.SMEM),
         ],
         out_specs=pl.BlockSpec(memory_space=pltpu.VMEM),
         scratch_shapes=[
+            pltpu.VMEM((slab, chi), BF),
             pltpu.VMEM((slab, chi, chi), BF),
             pltpu.VMEM((n, slab, slab, chi), BF),
             pltpu.VMEM((slab, chi, chi), BF),
@@ -231,7 +242,7 @@
             pltpu.VMEM((slab, chi), BF),
             pltpu.VMEM((LEVELS, chi, chi), BF),
             pltpu.VMEM((LEVELS, n, slab, chi), BF),
-            sem,
+            sem, sem,
             sem((CHUNKS,)), sem((CHUNKS,)),
             sem((LEVELS,)), sem((LEVELS,)),
             sem((LEVELS,)), sem((LEVELS,)),
@@ -240,7 +251,7 @@
         ],
         compiler_params=pltpu.CompilerParams(collective_id=0, has_side_effects=True),
     )(iso, leaf_ops[0, 0], jnp.transpose(charges, (1, 0, 2)), assign[0])
-    return result[None, None]
+    return result.astype(BF)[None, None]
 
 
 def solution(mesh):

time: 76.3 us -> 77.5 us (1.016)
  other arithmetic: 0 us -> 1.32 us
  local copies, waits for them, and re-layouts: 1.3 us -> 0 us
  Pallas kernels: 74.1 us -> 75.3 us
    broadcast_in_dim x0 -> x1, other arithmetic: none -> 1.32 us  [shards(): return result.astype(BF)[None, None]]
    unnamed x1 -> x0, local copies, waits for them, and re-layouts: 1.3 us -> none
    pallas_call x1, Pallas kernels: 74.1 us -> 75.3 us  [shards(): pl.pallas_call(functools.partial(kernel, n, leaves), out_shape=jax.ShapeD...]
where the time goes in v4:
time: 77.5 us; the launch traced here: 77.3 us
  Pallas kernels  75.3 us (97%)
  other arithmetic  1.32 us (2%)
    pallas_call x1, Pallas kernels, shards(): pl.pallas_call(functools.partial(kernel, n, leaves), out_shape=jax.ShapeD...  75.3 us

profile of v4, /device:TPU:2, one launch (start us, length us, event | category | flops | bytes accessed | tf_op | source)
XLA Modules:
  0.0 77.3 jit_solution(15566721540073431182)
XLA Ops:
  0.7 75.3 %shard_map.46 = f32[16,256]{1,0:T(8,128)} custom-call(bf16[16,256,256]{2,1,0:T(8,128)(2,1)} %bitcast.7, bf16[16,256]{1,0:T(8,128)(2,1)} %bitcast.8, s32[3,1,4]{2,1,0:T(1,128)} %bitcast.9, s32[1]{0:T(128)} %bitcast.6.assign), custom_call_target="tpu_custom_call" | custom-call | tf_op jit(solution)/shard_map/pallas_call | solution.py:218
  76.0 1.3 %convert_bitcast_fusion = bf16[1,1,16,256]{3,2,1,0:T(8,128)(2,1)} fusion(f32[16,256]{1,0:T(8,128)} %shard_map.46), kind=kLoop, calls=%fused_computation | loop fusion | flops 4096 | bytes 24576 | tf_op jit(solution)/shard_map/broadcast_in_dim | solution.py:254

commit v5 on v3

--- a/solution.py
+++ b/solution.py
@@ -10,7 +10,8 @@
 
 NBLK = 4
 LEVELS = 3
-CHUNKS = 4
+CHUNK_ROWS = (6, 5, 4, 1)
+CHUNKS = len(CHUNK_ROWS)
 BF = jnp.bfloat16
 F32 = jnp.float32
 MESH = pl.DeviceIdType.MESH
@@ -27,7 +28,7 @@
 ):
     slab, chi, _ = iso.shape
     block = chi // NBLK
-    per = slab // CHUNKS
+    starts = [sum(CHUNK_ROWS[:c]) for c in range(CHUNKS)]
     me = lax.axis_index("bond")
     slot = lax.axis_index("leaf")
 
@@ -106,15 +107,15 @@
     )
 
     def publish(src, level):
-        for at in steps:
-            if level > 0:
+        for at in others_at:
+            post(src, rbuf, level, r_send, r_recv, slot, at)
+        if level > 0:
+            for at in steps:
                 post(src, lbuf, level, l_send, l_recv, ahead(2**level), at)
-            if at != (0, 0):
-                post(src, rbuf, level, r_send, r_recv, slot, at)
         rbuf[level, mine] = src[...]
 
     def exchange(c):
-        part = pl.ds(c * per, per)
+        part = pl.ds(starts[c], CHUNK_ROWS[c])
 
         for at in others_at:
             to_dev = peer(at)
@@ -160,14 +161,14 @@
         scaled[...] = lbuf[level] * take_left
         if level == 0:
             for c in range(CHUNKS):
-                drain(mb.at[pl.ds(c * per, per), others], a2a_recv.at[c])
+                drain(mb.at[pl.ds(starts[c], CHUNK_ROWS[c]), others], a2a_recv.at[c])
 
                 def turn(b, carry):
                     ut[b] = mb[b].T
                     return carry
 
-                lax.fori_loop(c * per, (c + 1) * per, turn, 0, unroll=True)
-                contract(ut, mb, c * per, per)
+                lax.fori_loop(starts[c], starts[c] + CHUNK_ROWS[c], turn, 0, unroll=True)
+                contract(ut, mb, starts[c], CHUNK_ROWS[c])
         else:
             contract(ut, mb, 0, slab)
 
@@ -192,7 +193,7 @@
 
     hand_on.wait_send()
     for c in range(CHUNKS):
-        drain(mb.at[pl.ds(c * per, per), others], a2a_send.at[c])
+        drain(mb.at[pl.ds(starts[c], CHUNK_ROWS[c]), others], a2a_send.at[c])
     for level in range(LEVELS):
         drain(rbuf.at[level, others], r_send.at[level])
         drain(lbuf.at[level] if level > 0 else lbuf.at[level, others], l_send.at[level])

time: 76.3 us -> 78.1 us (1.024)
  Pallas kernels: 74.1 us -> 75.9 us
    pallas_call x1, Pallas kernels: 74.1 us -> 75.9 us  [shards(): pl.pallas_call(functools.partial(kernel, n, leaves), out_shape=jax.ShapeD...]
where the time goes in v5:
time: 78.1 us; the launch traced here: 77.9 us
  Pallas kernels  75.9 us (97%)
  local copies, waits for them, and re-layouts  1.3 us (2%)
    pallas_call x1, Pallas kernels, shards(): pl.pallas_call(functools.partial(kernel, n, leaves), out_shape=jax.ShapeD...  75.9 us

profile of v5, /device:TPU:2, one launch (start us, length us, event | category | flops | bytes accessed | tf_op | source)
XLA Modules:
  0.0 77.9 jit_solution(7030532240810412815)
XLA Ops:
  0.7 75.9 %shard_map.46 = bf16[16,256]{1,0:T(8,128)(2,1)} custom-call(bf16[16,256,256]{2,1,0:T(8,128)(2,1)} %bitcast.6, bf16[16,256]{1,0:T(8,128)(2,1)} %bitcast.8, s32[3,1,4]{2,1,0:T(1,128)} %bitcast.9, s32[1]{0:T(128)} %bitcast.5.assign), custom_call_target="tpu_custom_call" | custom-call | tf_op jit(solution)/shard_map/pallas_call | solution.py:209
  76.6 1.3 %copy.7 = bf16[1,1,16,256]{3,2,1,0:T(8,128)(2,1)} copy(bf16[1,1,16,256]{3,2,1,0:T(8,128)(2,1)} %bitcast.7) | data formatting | bytes 16384

commit v6 on v3

--- a/solution.py
+++ b/solution.py
@@ -106,11 +106,21 @@
     )
 
     def publish(src, level):
-        for at in steps:
-            if level > 0:
+        def own():
+            for at in others_at:
+                post(src, rbuf, level, r_send, r_recv, slot, at)
+
+        def parent():
+            for at in steps:
                 post(src, lbuf, level, l_send, l_recv, ahead(2**level), at)
-            if at != (0, 0):
-                post(src, rbuf, level, r_send, r_recv, slot, at)
+
+        if level == 1:
+            parent()
+            own()
+        else:
+            own()
+            if level > 1:
+                parent()
         rbuf[level, mine] = src[...]
 
     def exchange(c):

time: 76.3 us -> 76.5 us (level)
  no operation moved by 1% of the time
where the time goes in v6:
time: 76.5 us; the launch traced here: 76.2 us
  Pallas kernels  74.3 us (97%)
  local copies, waits for them, and re-layouts  1.3 us (2%)
    pallas_call x1, Pallas kernels, shards(): pl.pallas_call(functools.partial(kernel, n, leaves), out_shape=jax.ShapeD...  74.3 us

profile of v6, /device:TPU:2, one launch (start us, length us, event | category | flops | bytes accessed | tf_op | source)
XLA Modules:
  0.0 76.2 jit_solution(4370878128660521533)
XLA Ops:
  0.7 74.3 %shard_map.46 = bf16[16,256]{1,0:T(8,128)(2,1)} custom-call(bf16[16,256,256]{2,1,0:T(8,128)(2,1)} %bitcast.6, bf16[16,256]{1,0:T(8,128)(2,1)} %bitcast.8, s32[3,1,4]{2,1,0:T(1,128)} %bitcast.9, s32[1]{0:T(128)} %bitcast.5.assign), custom_call_target="tpu_custom_call" | custom-call | tf_op jit(solution)/shard_map/pallas_call | solution.py:218
  74.9 1.3 %copy.7 = bf16[1,1,16,256]{3,2,1,0:T(8,128)(2,1)} copy(bf16[1,1,16,256]{3,2,1,0:T(8,128)(2,1)} %bitcast.7) | data formatting | bytes 16384

commit v7 on v3

--- a/solution.py
+++ b/solution.py
@@ -49,8 +49,13 @@
 
     mine = rows(me)
 
-    load = pltpu.make_async_copy(iso, mm, load_sem)
-    load.start()
+    span = chi // NBLK
+    loads = [
+        pltpu.make_async_copy(iso.at[:, pl.ds(k * span, span)], mm.at[:, pl.ds(k * span, span)], load_sem.at[k])
+        for k in range(NBLK)
+    ]
+    for load in loads:
+        load.start()
 
     barrier = pltpu.get_barrier_semaphore()
 
@@ -63,19 +68,20 @@
                 barrier, inc=1, device_id=(ahead(leaves - 2**level), peer(at)), device_id_type=MESH
             )
 
-    row_block = lax.broadcasted_iota(jnp.int32, (chi, chi), 0) // block
-    col_block = lax.broadcasted_iota(jnp.int32, (chi, chi), 1) // block
-    total = jnp.zeros((chi, chi), jnp.int32) + charges[0, 0, (me * slab) // block]
+    down = lax.broadcasted_iota(jnp.int32, (chi, 1), 0) // block
+    across = lax.broadcasted_iota(jnp.int32, (1, chi), 1) // block
+    left_right = jnp.zeros((chi, 1), jnp.int32) + charges[0, 0, (me * slab) // block]
+    parent = jnp.zeros((1, chi), jnp.int32)
     for k in range(NBLK):
-        total = total + jnp.where(row_block == k, charges[1, 0, k], 0) - jnp.where(col_block == k, charges[2, 0, k], 0)
-    mask[...] = jnp.where((total & 3) == 0, 1.0, 0.0).astype(BF)
+        left_right = left_right + jnp.where(down == k, charges[1, 0, k], 0)
+        parent = parent + jnp.where(across == k, charges[2, 0, k], 0)
+    mask[...] = jnp.where(((left_right - parent) & 3) == 0, 1.0, 0.0).astype(BF)
 
     side = slab * slab
-    to = lax.broadcasted_iota(jnp.int32, (side, side), 0)
-    frm = lax.broadcasted_iota(jnp.int32, (side, side), 1)
-    perm[...] = jnp.where((to // slab == frm % slab) & (to % slab == frm // slab), 1.0, 0.0).astype(BF)
-
-    load.wait()
+    to = lax.broadcasted_iota(jnp.int32, (side, 1), 0)
+    frm = lax.broadcasted_iota(jnp.int32, (1, side), 1)
+    perm[...] = jnp.where(to // slab + to % slab * slab == frm, 1.0, 0.0).astype(BF)
+
 
     def prepare(e, carry):
         piece = mm[:, rows(e), :] * mask[rows(e), :][None]
@@ -84,7 +90,9 @@
         sendb[e] = turned.reshape(slab, slab, chi)
         return carry
 
-    lax.fori_loop(0, n, prepare, 0, unroll=4)
+    for k, load in enumerate(loads):
+        load.wait()
+        lax.fori_loop(k * n // NBLK, (k + 1) * n // NBLK, prepare, 0, unroll=True)
     mb[:, mine, :] = sendb[me]
 
     pl.semaphore_wait(barrier, n + n * (LEVELS - 1))
@@ -199,6 +207,12 @@
         drain(rsr.at[level, pl.ds(0, n - 1)], s_send.at[level])
 
 
+def place(src, dst, done):
+    copy = pltpu.make_async_copy(src, dst, done)
+    copy.start()
+    copy.wait()
+
+
 def shards(isometries, leaf_ops, charges, assign):
     iso = isometries[0]
     slab, chi, _ = iso.shape
@@ -231,7 +245,7 @@
             pltpu.VMEM((slab, chi), BF),
             pltpu.VMEM((LEVELS, chi, chi), BF),
             pltpu.VMEM((LEVELS, n, slab, chi), BF),
-            sem,
+            sem((NBLK,)),
             sem((CHUNKS,)), sem((CHUNKS,)),
             sem((LEVELS,)), sem((LEVELS,)),
             sem((LEVELS,)), sem((LEVELS,)),
@@ -240,6 +254,13 @@
         ],
         compiler_params=pltpu.CompilerParams(collective_id=0, has_side_effects=True),
     )(iso, leaf_ops[0, 0], jnp.transpose(charges, (1, 0, 2)), assign[0])
+    result = pl.pallas_call(
+        place,
+        out_shape=jax.ShapeDtypeStruct((slab, chi), BF),
+        in_specs=[pl.BlockSpec(memory_space=pl.ANY)],
+        out_specs=pl.BlockSpec(memory_space=pl.ANY),
+        scratch_shapes=[sem],
+    )(result)
     return result[None, None]
 
 

time: 76.3 us -> 76.2 us (level)
  Pallas kernels: 74.1 us -> 75.4 us
  local copies, waits for them, and re-layouts: 1.3 us -> 0 us
    pallas_call x0 -> x1, Pallas kernels: none -> 1.36 us  [shards(): pl.pallas_call(place, out_shape=jax.ShapeDtypeStruct((slab, chi), BF), in...]
    unnamed x1 -> x0, local copies, waits for them, and re-layouts: 1.3 us -> none
where the time goes in v7:
time: 76.2 us; the launch traced here: 76.1 us
  Pallas kernels  75.4 us (99%)
    pallas_call x1, Pallas kernels, shards(): pl.pallas_call(functools.partial(kernel, n, leaves), out_shape=jax.ShapeD...  74 us

profile of v7, /device:TPU:2, one launch (start us, length us, event | category | flops | bytes accessed | tf_op | source)
XLA Modules:
  0.0 76.1 jit_solution(3677198410150772731)
XLA Ops:
  0.7 74.0 %shard_map.46.src = bf16[16,256]{1,0:T(8,128)(2,1)} custom-call(bf16[16,256,256]{2,1,0:T(8,128)(2,1)} %bitcast.6, bf16[16,256]{1,0:T(8,128)(2,1)} %bitcast.7, s32[3,1,4]{2,1,0:T(1,128)} %bitcast.8, s32[1]{0:T(128)} %bitcast.5.assign), custom_call_target="tpu_custom_call" | custom-call | tf_op jit(solution)/shard_map/pallas_call | solution.py:222
  74.7 1.4 %shard_map.47 = bf16[16,256]{1,0:T(8,128)(2,1)} custom-call(bf16[16,256]{1,0:T(8,128)(2,1)} %shard_map.46.src), custom_call_target="tpu_custom_call" | custom-call | tf_op jit(solution)/shard_map/pallas_call | solution.py:257

commit v8 on v3

--- a/solution.py
+++ b/solution.py
@@ -11,6 +11,7 @@
 NBLK = 4
 LEVELS = 3
 CHUNKS = 4
+VMEM_MIB = 48
 BF = jnp.bfloat16
 F32 = jnp.float32
 MESH = pl.DeviceIdType.MESH
@@ -188,7 +189,7 @@
             xs[level] = whole.astype(BF)
             publish(xs.at[level], level + 1)
         else:
-            out[...] = whole.astype(BF)
+            out[...] = whole
 
     hand_on.wait_send()
     for c in range(CHUNKS):
@@ -197,6 +198,10 @@
         drain(rbuf.at[level, others], r_send.at[level])
         drain(lbuf.at[level] if level > 0 else lbuf.at[level, others], l_send.at[level])
         drain(rsr.at[level, pl.ds(0, n - 1)], s_send.at[level])
+
+
+def hbm(x):
+    return pltpu.with_memory_space_constraint(x, pltpu.HBM)
 
 
 def shards(isometries, leaf_ops, charges, assign):
@@ -207,7 +212,7 @@
     sem = pltpu.SemaphoreType.DMA
     result = pl.pallas_call(
         functools.partial(kernel, n, leaves),
-        out_shape=jax.ShapeDtypeStruct((slab, chi), BF),
+        out_shape=jax.ShapeDtypeStruct((slab, chi), F32),
         in_specs=[
             pl.BlockSpec(memory_space=pl.ANY),
             pl.BlockSpec(memory_space=pltpu.VMEM),
@@ -238,9 +243,9 @@
             sem, sem,
             sem((LEVELS,)), sem((LEVELS,)),
         ],
-        compiler_params=pltpu.CompilerParams(collective_id=0, has_side_effects=True),
-    )(iso, leaf_ops[0, 0], jnp.transpose(charges, (1, 0, 2)), assign[0])
-    return result[None, None]
+        compiler_params=pltpu.CompilerParams(collective_id=0, has_side_effects=True, vmem_limit_bytes=VMEM_MIB * 2**20),
+    )(hbm(iso), hbm(leaf_ops[0, 0]), hbm(jnp.transpose(charges, (1, 0, 2))), assign[0])
+    return result.astype(BF)[None, None]
 
 
 def solution(mesh):

time: 76.3 us -> 75 us (0.983)
  local copies, waits for them, and re-layouts: 1.3 us -> 0 us
    unnamed x1 -> x0, local copies, waits for them, and re-layouts: 1.3 us -> none
where the time goes in v8:
time: 75 us; the launch traced here: 74.8 us
  Pallas kernels  73.5 us (98%)
    pallas_call x1, Pallas kernels, shards(): pl.pallas_call(functools.partial(kernel, n, leaves), out_shape=jax.ShapeD...  73.5 us

profile of v8, /device:TPU:2, one launch (start us, length us, event | category | flops | bytes accessed | tf_op | source)
XLA Modules:
  0.0 74.8 jit_solution(16005252230872753139)
XLA Ops:
  0.7 73.5 %shard_map.46 = f32[16,256]{1,0:T(8,128)S(1)} custom-call(bf16[16,256,256]{2,1,0:T(8,128)(2,1)} %bitcast.7, bf16[16,256]{1,0:T(8,128)(2,1)} %bitcast.8, s32[3,1,4]{2,1,0:T(1,128)} %bitcast.9, s32[1]{0:T(128)} %bitcast.6.assign), custom_call_target="tpu_custom_call" | custom-call | tf_op jit(solution)/shard_map/pallas_call | solution.py:213
  74.2 0.6 convert_bitcast_fusion
